TPU v7x, 32 devices: a whole 2x2x4 slice. The times are simulated.
32 devices in a mesh: slab: 4 (over x, core), kt: 8 (over z, y).
Axes of the slice: x: 2, y: 2, z: 4, core: 2. Of those that a mesh axis runs over, the one named last changes fastest.
Arguments:
- energies: float32 [4], replicated, may hold values from -0.5 to 0.1
- onsite: float32 [8, 4, 384], P('kt', 'slab'), may hold values from -3.5 to -2.5
- hamiltonian: bfloat16 [8, 4, 2, 384, 384], P('kt', 'slab'), may hold values from -0.109375 to 0.109375
- hopping: bfloat16 [8, 4, 2, 384, 384], P('kt', 'slab'), may hold values from -0.15625 to 0.15625
- contact: bfloat16 [8, 2, 384, 384], P('kt'), may hold values from -2 to 2
- previous: bfloat16 [8, 4, 4, 2, 2, 384, 384], P('kt', None, 'slab'), may hold values from -4 to 4
- neighbours: int32 [8, 2], P('kt'), may hold values from 0 to 7, as said below
- mode_index: int32 [8, 2], P('kt'), may hold values from 0 to 3
- mode_strength: float32 [4], replicated, may hold values from 0.25 to 1
Outputs:
- retarded: bfloat16 [8, 4, 4, 2, 384, 384], P('kt', None, 'slab')
- lesser: bfloat16 [8, 4, 4, 2, 384, 384], P('kt', None, 'slab')
Inputs may be any that keep to these rules, and one draw needn't show every extreme that they name: neighbours[k, 0] is k - 1 or k - 2 and neighbours[k, 1] is k + 1 or k + 2, modulo 8.
All inputs are finite; a program needn't handle non-finite values.
Results may differ from a plain program's by a relative error of at most 0.017.
Values may be sent and summed in bfloat16 or wider, within the bound.
A program may use at most 128 MiB of HBM per device.

v0:
```python
import jax
import jax.numpy as jnp
from jax import lax
from jax.sharding import PartitionSpec as P

broaden = 0.05
fermi_level = 0.0
thermal = 0.1


def from_behind(value, axis, by):
    peers = lax.axis_size(axis)
    return lax.ppermute(value, axis, [(i, (i + by) % peers) for i in range(peers)])


def as_sent(value):
    return jax.tree.map(lambda a: a.astype(jnp.bfloat16) if a.dtype == jnp.float32 else a, value)


def combine(pieces):
    real_part = pieces[..., 0, 0, :, :] - pieces[..., 1, 1, :, :]
    imaginary_part = pieces[..., 0, 1, :, :] + pieces[..., 1, 0, :, :]
    return jnp.stack([real_part, imaginary_part], axis=-3)


def complex_mul(first_op, second_op):
    return combine(
        jnp.einsum("pij,qjk->pqik", first_op, second_op, preferred_element_type=jnp.float32)
    )


def adjoint(matrix):
    return jnp.stack([matrix[0].T, -matrix[1].T])


def slab_update(boundary, energy, levels, hamilton, coupling, phonon):
    moved_blocks = combine(
        jnp.einsum("pij,sqjk->spqik", coupling, boundary, preferred_element_type=jnp.float32)
    ).astype(jnp.bfloat16)
    self_both = combine(
        jnp.einsum(
            "spij,qjk->spqik", moved_blocks, adjoint(coupling), preferred_element_type=jnp.float32
        )
    )
    self_retarded = self_both[0]
    self_lesser = self_both[1]
    identity = jnp.eye(levels.shape[0], dtype=jnp.float32)
    system_real = (
        (energy - levels)[:, None] * identity
        - hamilton[0].astype(jnp.float32)
        - self_retarded[0]
        - phonon[0, 0]
    )
    system_imaginary = (
        broaden * identity - hamilton[1].astype(jnp.float32) - self_retarded[1] - phonon[0, 1]
    )
    diagonal_real = jnp.diagonal(system_real)
    diagonal_imaginary = jnp.diagonal(system_imaginary)
    modulus = diagonal_real * diagonal_real + diagonal_imaginary * diagonal_imaginary
    inverse_real = diagonal_real / modulus
    inverse_imaginary = -diagonal_imaginary / modulus
    scaled_real = (
        inverse_real[:, None] * system_real - inverse_imaginary[:, None] * system_imaginary
    )
    scaled_imaginary = (
        inverse_real[:, None] * system_imaginary + inverse_imaginary[:, None] * system_real
    )
    sandwich_real = (
        scaled_real * inverse_real[None, :] - scaled_imaginary * inverse_imaginary[None, :]
    )
    sandwich_imaginary = (
        scaled_real * inverse_imaginary[None, :] + scaled_imaginary * inverse_real[None, :]
    )
    first_guess = jnp.stack(
        [
            2.0 * jnp.diag(inverse_real) - sandwich_real,
            2.0 * jnp.diag(inverse_imaginary) - sandwich_imaginary,
        ]
    )
    first_rounded = first_guess.astype(jnp.bfloat16)
    system_rounded = jnp.stack([system_real, system_imaginary]).astype(jnp.bfloat16)
    product = complex_mul(system_rounded, first_rounded).astype(jnp.bfloat16)
    retarded = (2.0 * first_guess - complex_mul(first_rounded, product)).astype(jnp.bfloat16)
    source = (phonon[1] + self_lesser).astype(jnp.bfloat16)
    halfway = complex_mul(retarded, source).astype(jnp.bfloat16)
    lesser = complex_mul(halfway, adjoint(retarded)).astype(jnp.bfloat16)
    return (retarded, lesser)


def sweep_energy(boundary, energy, phonon, level_all, hamilton_all, coupling_all):
    slab_count = level_all.shape[0]
    retarded_list = [None] * slab_count
    lesser_list = [None] * slab_count
    for slab_num in reversed(range(slab_count)):
        ret_block, les_block = slab_update(
            boundary,
            energy,
            level_all[slab_num],
            hamilton_all[slab_num],
            coupling_all[slab_num],
            phonon[slab_num],
        )
        retarded_list[slab_num] = ret_block
        lesser_list[slab_num] = les_block
        boundary = jnp.stack([ret_block, les_block])
    return (jnp.stack(retarded_list), jnp.stack(lesser_list), boundary)


def cycle_phonon(blocks, neighbours, mode_index, mode_strength):
    nearest = [from_behind(blocks, "kt", offset) for offset in (1, -1)]
    farther = [from_behind(blocks, "kt", offset) for offset in (2, -2)]
    kpoint = lax.axis_index("kt")
    cycle_size = lax.axis_size("kt")
    neighbour_pair = neighbours[0]
    behind = jnp.where(neighbour_pair[0] == (kpoint - 1) % cycle_size, nearest[0], farther[0])
    forward = jnp.where(neighbour_pair[1] == (kpoint + 1) % cycle_size, nearest[1], farther[1])
    mode_table = jnp.arange(mode_strength.shape[0], dtype=jnp.int32)
    strength = jnp.sum(
        jnp.where(mode_index[0][:, None] == mode_table[None, :], mode_strength[None, :], 0.0),
        axis=1,
    )
    return strength[0] * behind[0].astype(jnp.float32) + strength[1] * forward[0].astype(
        jnp.float32
    )


def starting_blocks(contact, energy_list):
    contact_block = contact[0]
    contact_float = contact_block.astype(jnp.float32)
    skew_part = jnp.stack(
        [contact_float[0] - contact_float[0].T, contact_float[1] + contact_float[1].T]
    )
    occupation = 1.0 / (1.0 + jnp.exp((energy_list - fermi_level) / thermal))
    energy_count = energy_list.shape[0]
    contact_lesser = (-occupation[:, None, None, None] * skew_part).astype(jnp.bfloat16)
    return jnp.stack(
        [jnp.broadcast_to(contact_block, (energy_count,) + contact_block.shape), contact_lesser],
        axis=1,
    )


def body(
    energies, onsite, hamiltonian, hopping, contact, previous, neighbours, mode_index, mode_strength
):
    position = lax.axis_index("slab")
    regrouped = lax.all_to_all(previous, "slab", split_axis=1, concat_axis=2, tiled=True)
    phonon_all = cycle_phonon(regrouped, neighbours, mode_index, mode_strength)
    level_whole = lax.all_gather(onsite, "slab", axis=1, tiled=True)
    hamilton_whole, coupling_whole = (
        lax.all_gather(hamiltonian, "slab", axis=1, tiled=True),
        lax.all_gather(hopping, "slab", axis=1, tiled=True),
    )
    local_count = regrouped.shape[1]
    local_energies = lax.dynamic_slice_in_dim(energies, position * local_count, local_count, 0)
    initial = starting_blocks(contact, local_energies)

    def run_whole(boundary, energy, phonon):
        return sweep_energy(
            boundary, energy, phonon, level_whole[0], hamilton_whole[0], coupling_whole[0]
        )

    retarded_local, lesser_local, unused = jax.vmap(run_whole)(initial, local_energies, phonon_all)
    retarded_all, lesser_all = (
        lax.all_to_all(
            as_sent(retarded_local[None]), "slab", split_axis=2, concat_axis=1, tiled=True
        ),
        lax.all_to_all(
            as_sent(lesser_local[None]), "slab", split_axis=2, concat_axis=1, tiled=True
        ),
    )
    return (retarded_all, lesser_all)


def solution(mesh):
    in_specs = (
        P(),
        P("kt", "slab", None),
        P("kt", "slab", None, None, None),
        P("kt", "slab", None, None, None),
        P("kt", None, None, None),
        P("kt", None, "slab", None, None, None, None),
        P("kt", None),
        P("kt", None),
        P(),
    )
    out_specs = (P("kt", None, "slab", None, None, None), P("kt", None, "slab", None, None, None))
    return jax.shard_map(body, mesh=mesh, in_specs=in_specs, out_specs=out_specs, check_vma=False)
```

profile of v0, /device:TPU:0, one launch (start us, length us, event | category | flops | bytes accessed | tf_op | source)
XLA Modules:
  0.0 600.2 jit_solution(12964308768972763994)
XLA Ops:
  7.9 6.7 %copy.286 = bf16[1,4,1,2,2,384,384]{5,6,4,3,2,0,1:T(8,128)(2,1)} copy(bf16[1,4,1,2,2,384,384]{6,5,4,3,2,1,0:T(8,128)(2,1)} %param.14) | data formatting | bytes 9437184 | tf_op args[5]
  14.6 5.1 all-to-all-start
  20.4 77.7 %all-to-all-done = bf16[1,4,1,2,2,384,384]{5,6,4,3,2,0,1:T(8,128)(2,1)} async-done(((bf16[1,4,1,2,2,384,384]{5,6,4,3,2,0,1:T(8,128)(2,1)}), bf16[1,4,1,2,2,384,384]{5,6,4,3,2,0,1:T(8,128)(2,1)}, u32[]{:S(2)}, u32[]{:S(2)}) %all-to-all-start) | async-done | bytes 4718624 | tf_op jit(solution)/shard_map/all_to_all | solution.py:146
  101.1 3.2 collective-permute-start.2
  111.6 5.2 all_gather.9
  119.0 1.8 fusion.322
  128.1 2.5 convolution_bitcast_fusion.7
  137.2 68.8 %collective-permute-done = bf16[1,1,4,2,2,384,384]{5,6,4,3,2,1,0:T(8,128)(2,1)} collective-permute-done((bf16[1,1,4,2,2,384,384]{5,6,4,3,2,1,0:T(8,128)(2,1)}, bf16[1,1,4,2,2,384,384]{5,6,4,3,2,1,0:T(8,128)(2,1)}, u32[]{:S(2)}, u32[]{:S(2)}) %collective-permute-start) | collective-permute-done | bytes 4718624 | tf_op jit(solution)/shard_map/ppermute | solution.py:13
  206.4 99.2 %collective-permute-done.2 = bf16[1,1,4,2,2,384,384]{5,6,4,3,2,1,0:T(8,128)(2,1)} collective-permute-done((bf16[1,1,4,2,2,384,384]{5,6,4,3,2,1,0:T(8,128)(2,1)}, bf16[1,1,4,2,2,384,384]{5,6,4,3,2,1,0:T(8,128)(2,1)}, u32[]{:S(2)}, u32[]{:S(2)}) %collective-permute-start.2) | collective-permute-done | bytes 4718624 | tf_op jit(solution)/shard_map/ppermute | solution.py:13
  305.6 101.7 %collective-permute-done.3 = bf16[1,1,4,2,2,384,384]{5,6,4,3,2,1,0:T(8,128)(2,1)} collective-permute-done((bf16[1,1,4,2,2,384,384]{5,6,4,3,2,1,0:T(8,128)(2,1)}, bf16[1,1,4,2,2,384,384]{5,6,4,3,2,1,0:T(8,128)(2,1)}, u32[]{:S(2)}, u32[]{:S(2)}) %collective-permute-start.3) | collective-permute-done | bytes 4718624 | tf_op jit(solution)/shard_map/ppermute | solution.py:13
  407.3 12.0 %add_bitcast_fusion = f32[1,4,2,2,384,384]{4,5,3,2,1,0:T(8,128)} fusion(bf16[1,1,4,2,2,384,384]{5,6,4,3,2,1,0:T(8,128)(2,1)} %collective-permute-done.2, bf16[1,1,4,2,2,384,384]{5,6,4,3,2,1,0:T(8,128)(2,1)} %collective-permute-done.3, f32[]{:T(128)} %bitcast.80, bf16[1,1,4,2,2,384,384]{5,6,4,3,2,1,0:T(8,128)(2,1)} %collective-permute-done, ...), kind=kLoop, calls=%fused_computation.8 | loop fusion | flops 16515072 | bytes 28311562 | tf_op jit(solution)/shard_map/add | solution.py:122
  419.3 6.6 %slice_bitcast_fusion = (f32[1,2,2,384,384]{3,4,2,1,0:T(8,128)S(1)}, f32[1,2,2,384,384]{3,4,2,1,0:T(8,128)}, f32[1,2,2,384,384]{3,4,2,1,0:T(8,128)}, f32[1,1,2,2,384,384]{4,5,3,2,1,0:T(8,128)S(1)}) fusion(f32[1,4,2,2,384,384]{4,5,3,2,1,0:T(8,128)} %add_bitcast_fusion), kind=kLoop, calls=%fused_computation.9 | loop fusion | bytes 18874368 | tf_op jit(solution)/shard_map/vmap()/squeeze | solution.py:101
  429.8 5.1 gather_fusion
  434.9 4.5 gather_fusion.1
  448.2 2.5 convolution_bitcast_fusion.5
  457.6 3.5 gather_fusion.3
  461.1 4.7 gather_fusion.2
  474.6 2.5 convolution_bitcast_fusion.3
  484.0 3.5 gather_fusion.5
  487.5 3.7 gather_fusion.4
  499.4 2.5 convolution_bitcast_fusion.1
  507.8 3.5 gather_fusion.7
  511.3 3.5 gather_fusion.6
  514.8 1.6 subtract_subtract_fusion
  523.7 1.6 maximum_bitcast_fusion.1
  525.3 4.6 all-to-all-start.2
  531.4 1.8 maximum_bitcast_fusion
  533.1 25.3 %all-to-all-done.2 = bf16[1,1,4,2,384,384]{4,5,3,1,0,2:T(8,128)(2,1)} async-done(((bf16[1,1,4,2,384,384]{4,5,3,1,0,2:T(8,128)(2,1)}), bf16[1,1,4,2,384,384]{4,5,3,1,0,2:T(8,128)(2,1)}, u32[]{:S(2)}, u32[]{:S(2)}) %all-to-all-start.2) | async-done | bytes 2359328 | tf_op jit(solution)/shard_map/all_to_all | solution.py:167
  558.5 3.6 all-to-all-start.1
  562.1 4.3 copy.358
  566.4 24.2 %all-to-all-done.1 = bf16[1,1,4,2,384,384]{4,5,3,1,0,2:T(8,128)(2,1)S(1)} async-done(((bf16[1,1,4,2,384,384]{4,5,3,1,0,2:T(8,128)(2,1)}), bf16[1,1,4,2,384,384]{4,5,3,1,0,2:T(8,128)(2,1)S(1)}, u32[]{:S(2)}, u32[]{:S(2)}) %all-to-all-start.1) | async-done | bytes 2359328 | tf_op jit(solution)/shard_map/all_to_all | solution.py:164
  590.5 2.6 copy.357
  (279 shorter events, 83.3 us)
Async XLA Ops:
  7.2 111.8 %all-gather.3.cloned.1.call-start = ((), (), s32[]{:S(2)}) async-start(), calls=%async_computation.3 | async-start | bytes 2949120 | tf_op jit(solution)/shard_map/all_gather | solution.py:150
  14.6 90.3 %copy-start.54 = (bf16[1,2,384,384]{3,2,1,0:T(8,128)(2,1)S(1)}, bf16[1,2,384,384]{3,2,1,0:T(8,128)(2,1)}, u32[]{:S(2)}) copy-start(bf16[1,2,384,384]{3,2,1,0:T(8,128)(2,1)} %param.13) | copy-start | bytes 1769476
  14.6 83.5 %all-to-all-start = ((bf16[1,4,1,2,2,384,384]{5,6,4,3,2,0,1:T(8,128)(2,1)}), bf16[1,4,1,2,2,384,384]{5,6,4,3,2,0,1:T(8,128)(2,1)}, u32[]{:S(2)}, u32[]{:S(2)}) async-start(bf16[1,4,1,2,2,384,384]{5,6,4,3,2,0,1:T(8,128)(2,1)} %copy.286), calls=%async_computation | async-start | bytes 9437184 | tf_op jit(solution)/shard_map/all_to_all | solution.py:146
  19.6 108.4 %all-gather.5.cloned.1.call-start = ((), (), s32[]{:S(2)}) async-start(), calls=%async_computation.4 | async-start | bytes 2949120 | tf_op jit(solution)/shard_map/all_gather | solution.py:151
  98.1 107.9 %collective-permute-start = (bf16[1,1,4,2,2,384,384]{5,6,4,3,2,1,0:T(8,128)(2,1)}, bf16[1,1,4,2,2,384,384]{5,6,4,3,2,1,0:T(8,128)(2,1)}, u32[]{:S(2)}, u32[]{:S(2)}) collective-permute-start(bf16[1,1,4,2,2,384,384]{5,6,4,3,2,1,0:T(8,128)(2,1)} %bitcast.79), channel_id=1, source_target_pairs={{0,1},{1,2},{2,3},{3,4},{4,5},{5,6},{6,7},{7,0},{8,9},{9,10},{10,1... | collective-permute-start | bytes 14155784 | tf_op jit(solution)/shard_map/ppermute | solution.py:13
  99.6 106.8 %collective-permute-start.1 = (bf16[1,1,4,2,2,384,384]{5,6,4,3,2,1,0:T(8,128)(2,1)}, bf16[1,1,4,2,2,384,384]{5,6,4,3,2,1,0:T(8,128)(2,1)}, u32[]{:S(2)}, u32[]{:S(2)}) collective-permute-start(bf16[1,1,4,2,2,384,384]{5,6,4,3,2,1,0:T(8,128)(2,1)} %bitcast.79), channel_id=1, source_target_pairs={{0,2},{1,3},{2,4},{3,5},{4,6},{5,7},{6,0},{7,1},{8,10},{9,11},{10,... | collective-permute-start | bytes 14155784 | tf_op jit(solution)/shard_map/ppermute | solution.py:13
  101.1 204.6 %collective-permute-start.2 = (bf16[1,1,4,2,2,384,384]{5,6,4,3,2,1,0:T(8,128)(2,1)}, bf16[1,1,4,2,2,384,384]{5,6,4,3,2,1,0:T(8,128)(2,1)}, u32[]{:S(2)}, u32[]{:S(2)}) collective-permute-start(bf16[1,1,4,2,2,384,384]{5,6,4,3,2,1,0:T(8,128)(2,1)} %bitcast.79), channel_id=1, source_target_pairs={{0,7},{1,0},{2,1},{3,2},{4,3},{5,4},{6,5},{7,6},{8,15},{9,8},{10,9... | collective-permute-start | bytes 14155784 | tf_op jit(solution)/shard_map/ppermute | solution.py:13
  104.3 303.0 %collective-permute-start.3 = (bf16[1,1,4,2,2,384,384]{5,6,4,3,2,1,0:T(8,128)(2,1)}, bf16[1,1,4,2,2,384,384]{5,6,4,3,2,1,0:T(8,128)(2,1)}, u32[]{:S(2)}, u32[]{:S(2)}) collective-permute-start(bf16[1,1,4,2,2,384,384]{5,6,4,3,2,1,0:T(8,128)(2,1)} %bitcast.79), channel_id=1, source_target_pairs={{0,6},{1,7},{2,0},{3,1},{4,2},{5,3},{6,4},{7,5},{8,14},{9,15},{10,... | collective-permute-start | bytes 14155784 | tf_op jit(solution)/shard_map/ppermute | solution.py:13
  108.0 3.5 copy-start.74
  108.1 8.7 %copy-start.76 = (f32[4]{0:T(128)S(1)}, f32[4]{0:T(128)}, u32[]{:S(2)}) copy-start(f32[4]{0:T(128)} %param.17) | copy-start | bytes 52
  108.1 8.7 %copy-start.77 = (s32[1,2]{1,0:T(1,128)S(1)}, s32[1,2]{1,0:T(1,128)}, u32[]{:S(2)}) copy-start(s32[1,2]{1,0:T(1,128)} %param.16) | copy-start | bytes 28
  137.2 288.9 %copy-start.22 = (f32[1,2,384,384]{2,3,1,0:T(8,128)}, f32[1,2,384,384]{2,3,1,0:T(8,128)S(1)}, u32[]{:S(2)}) copy-start(f32[1,2,384,384]{2,3,1,0:T(8,128)S(1)} %fusion.7) | copy-start | bytes 3538948
  426.0 2.2 copy-start.4
  434.9 5.2 copy-start.55
  443.2 2.1 copy-start.7
  447.5 3.1 copy-start.28
  453.5 2.5 copy-start.2
  453.5 2.5 copy-start.50
  453.5 2.6 copy-start.51
  461.1 5.3 copy-start.56
  473.9 3.2 copy-start.30
  479.9 2.5 copy-start
  479.9 2.5 copy-start.48
  479.9 2.6 copy-start.49
  487.5 3.7 copy-start.57
  498.7 3.2 copy-start.32
  518.3 2.9 copy-start.24
  518.3 2.9 copy-start.26
  525.3 4.7 copy-start.25
  525.3 4.7 copy-start.27
  525.3 33.2 %all-to-all-start.2 = ((bf16[1,1,4,2,384,384]{4,5,3,1,0,2:T(8,128)(2,1)}), bf16[1,1,4,2,384,384]{4,5,3,1,0,2:T(8,128)(2,1)}, u32[]{:S(2)}, u32[]{:S(2)}) async-start(bf16[1,1,4,2,384,384]{4,5,3,1,0,2:T(8,128)(2,1)} %maximum_bitcast_fusion.1), calls=%async_computation.2 | async-start | bytes 4718592 | tf_op jit(solution)/shard_map/all_to_all | solution.py:167
  558.5 32.1 %all-to-all-start.1 = ((bf16[1,1,4,2,384,384]{4,5,3,1,0,2:T(8,128)(2,1)}), bf16[1,1,4,2,384,384]{4,5,3,1,0,2:T(8,128)(2,1)S(1)}, u32[]{:S(2)}, u32[]{:S(2)}) async-start(bf16[1,1,4,2,384,384]{4,5,3,1,0,2:T(8,128)(2,1)} %maximum_bitcast_fusion), calls=%async_computation.1 | async-start | bytes 4718592 | tf_op jit(solution)/shard_map/all_to_all | solution.py:164
  (55 other events, 69.6 us)
Sparse Core Ops, SparseCore 0:
  9.5 38.0 all-gather.2
  49.2 35.9 all-gather.4
where the time goes:
time: 610 us; the launch traced here: 600 us
  waiting for transfers between devices  399 us (65%)
  local copies, waits for them, and re-layouts  91.8 us (15%)
  other arithmetic  38.7 us (6%)
  matrix products  28 us (5%)
  starting transfers between devices  20.2 us (3%)
  between operations  17.6 us (3%)
    ppermute x4, waiting for transfers between devices, from_behind(): lax.ppermute(value, axis, [(i, (i + by) % peers) for i in range(peers)])  270 us
    all_to_all x1, waiting for transfers between devices, body(): lax.all_to_all(previous, 'slab', split_axis=1, concat_axis=2, tiled=True)  77.7 us
    unnamed x168, local copies, waits for them, and re-layouts  47 us
    all_to_all x1, waiting for transfers between devices, body(): lax.all_to_all(as_sent(lesser_local[None]), 'slab', split_axis=2, concat_...  25.3 us
    all_to_all x1, waiting for transfers between devices, body(): lax.all_to_all(as_sent(retarded_local[None]), 'slab', split_axis=2, conca...  24.2 us
    gather x4, local copies, waits for them, and re-layouts, slab_update(): diagonal_real = jnp.diagonal(system_real)  16.9 us
    gather x4, local copies, waits for them, and re-layouts, slab_update(): diagonal_imaginary = jnp.diagonal(system_imaginary)  14.9 us
    dot_general x16, matrix products, complex_mul(): jnp.einsum('pij,qjk->pqik', first_op, second_op, preferred_element_type=j...  12.6 us
  transfers between devices with their start and end apart: 9, of which 7 were waited for; matrix products, arithmetic and copies ran while one was open for 6% of the time, Pallas kernels for 0%

commit v1 on v0

--- a/solution.py
+++ b/solution.py
@@ -6,6 +6,28 @@
 broaden = 0.05
 fermi_level = 0.0
 thermal = 0.1
+
+
+def in_blocks(x, dim, length):
+    before, after = (x.shape[:dim], x.shape[dim + 1 :])
+    return jnp.moveaxis(x.reshape(*before, length, -1, *after), dim, 0)
+
+
+def laid_out(tiles, dim):
+    tiles = jnp.moveaxis(tiles, 0, dim)
+    lengths = tiles.shape
+    return tiles.reshape(*lengths[:dim], lengths[dim] * lengths[dim + 1], *lengths[dim + 2 :])
+
+
+def exchange_in_pairs(x, axis, split_dim, concat_dim):
+    peers, index = (lax.axis_size(axis), lax.axis_index(axis))
+    pieces = in_blocks(x, split_dim, peers)
+    finished = [pieces[index]]
+    for step in range(1, peers):
+        sent = pieces[index ^ step]
+        finished.append(lax.ppermute(sent, axis, [(i, i ^ step) for i in range(peers)]))
+    pieces = jnp.stack(finished)[index ^ jnp.arange(peers)]
+    return laid_out(pieces, concat_dim)
 
 
 def from_behind(value, axis, by):
@@ -164,9 +186,7 @@
         lax.all_to_all(
             as_sent(retarded_local[None]), "slab", split_axis=2, concat_axis=1, tiled=True
         ),
-        lax.all_to_all(
-            as_sent(lesser_local[None]), "slab", split_axis=2, concat_axis=1, tiled=True
-        ),
+        exchange_in_pairs(as_sent(lesser_local[None]), "slab", 2, 1),
     )
     return (retarded_all, lesser_all)
 

time: 610 us -> 608 us (level)
    ppermute x0 -> x3, waiting for transfers between devices: none -> 44.9 us  [exchange_in_pairs(): lax.ppermute(sent, axis, [(i, i ^ step) for i in range(peers)])]
    all_to_all x1 -> x0, waiting for transfers between devices: 25.3 us -> none  [body(): lax.all_to_all(as_sent(lesser_local[None]), 'slab', split_axis=2, concat_...]
    all_to_all x1, waiting for transfers between devices: 24.2 us -> 0.01 us  [body(): lax.all_to_all(as_sent(retarded_local[None]), 'slab', split_axis=2, conca...]
    unnamed x168 -> x171, local copies, waits for them, and re-layouts: 47 us -> 45.2 us
  transfers between devices with their start and end apart: 9 -> 11, of which waited for: 7 -> 7; matrix products, arithmetic and copies ran while one was open for 6% -> 6% of each run, Pallas kernels for 0% -> 0%
where the time goes in v1:
time: 608 us; the launch traced here: 599 us
  waiting for transfers between devices  394 us (65%)
  local copies, waits for them, and re-layouts  95.6 us (16%)
  other arithmetic  39.1 us (6%)
  matrix products  28 us (5%)
  starting transfers between devices  19 us (3%)
  between operations  17.8 us (3%)
    ppermute x4, waiting for transfers between devices, from_behind(): lax.ppermute(value, axis, [(i, (i + by) % peers) for i in range(peers)])  270 us
    all_to_all x1, waiting for transfers between devices, body(): lax.all_to_all(previous, 'slab', split_axis=1, concat_axis=2, tiled=True)  77.7 us
    unnamed x171, local copies, waits for them, and re-layouts  45.2 us
    ppermute x3, waiting for transfers between devices, exchange_in_pairs(): lax.ppermute(sent, axis, [(i, i ^ step) for i in range(peers)])  44.9 us
    gather x4, local copies, waits for them, and re-layouts, slab_update(): diagonal_real = jnp.diagonal(system_real)  16.9 us
    gather x4, local copies, waits for them, and re-layouts, slab_update(): diagonal_imaginary = jnp.diagonal(system_imaginary)  15 us
    dot_general x16, matrix products, complex_mul(): jnp.einsum('pij,qjk->pqik', first_op, second_op, preferred_element_type=j...  12.6 us
  transfers between devices with their start and end apart: 11, of which 7 were waited for; matrix products, arithmetic and copies ran while one was open for 6% of the time, Pallas kernels for 0%

profile of v1, /device:TPU:0, one launch (start us, length us, event | category | flops | bytes accessed | tf_op | source)
XLA Modules:
  0.0 598.6 jit_solution(15862127723592241607)
XLA Ops:
  7.9 6.7 %copy.369 = bf16[1,4,1,2,2,384,384]{5,6,4,3,2,0,1:T(8,128)(2,1)} copy(bf16[1,4,1,2,2,384,384]{6,5,4,3,2,1,0:T(8,128)(2,1)} %param.14) | data formatting | bytes 9437184 | tf_op args[5]
  14.6 5.1 all-to-all-start
  20.4 77.7 %all-to-all-done = bf16[1,4,1,2,2,384,384]{5,6,4,3,2,0,1:T(8,128)(2,1)} async-done(((bf16[1,4,1,2,2,384,384]{5,6,4,3,2,0,1:T(8,128)(2,1)}), bf16[1,4,1,2,2,384,384]{5,6,4,3,2,0,1:T(8,128)(2,1)}, u32[]{:S(2)}, u32[]{:S(2)}) %all-to-all-start) | async-done | bytes 4718624 | tf_op jit(solution)/shard_map/all_to_all | solution.py:168
  101.1 3.2 collective-permute-start.2
  111.7 5.2 all_gather.9
  119.1 1.9 fusion.323
  128.2 2.5 convolution_bitcast_fusion.7
  137.3 68.7 %collective-permute-done = bf16[1,1,4,2,2,384,384]{5,6,4,3,2,1,0:T(8,128)(2,1)} collective-permute-done((bf16[1,1,4,2,2,384,384]{5,6,4,3,2,1,0:T(8,128)(2,1)}, bf16[1,1,4,2,2,384,384]{5,6,4,3,2,1,0:T(8,128)(2,1)}, u32[]{:S(2)}, u32[]{:S(2)}) %collective-permute-start) | collective-permute-done | bytes 4718624 | tf_op jit(solution)/shard_map/ppermute | solution.py:35
  206.4 99.2 %collective-permute-done.2 = bf16[1,1,4,2,2,384,384]{5,6,4,3,2,1,0:T(8,128)(2,1)} collective-permute-done((bf16[1,1,4,2,2,384,384]{5,6,4,3,2,1,0:T(8,128)(2,1)}, bf16[1,1,4,2,2,384,384]{5,6,4,3,2,1,0:T(8,128)(2,1)}, u32[]{:S(2)}, u32[]{:S(2)}) %collective-permute-start.2) | collective-permute-done | bytes 4718624 | tf_op jit(solution)/shard_map/ppermute | solution.py:35
  305.6 101.7 %collective-permute-done.3 = bf16[1,1,4,2,2,384,384]{5,6,4,3,2,1,0:T(8,128)(2,1)} collective-permute-done((bf16[1,1,4,2,2,384,384]{5,6,4,3,2,1,0:T(8,128)(2,1)}, bf16[1,1,4,2,2,384,384]{5,6,4,3,2,1,0:T(8,128)(2,1)}, u32[]{:S(2)}, u32[]{:S(2)}) %collective-permute-start.3) | collective-permute-done | bytes 4718624 | tf_op jit(solution)/shard_map/ppermute | solution.py:35
  407.3 12.0 %add_bitcast_fusion = f32[1,4,2,2,384,384]{4,5,3,2,1,0:T(8,128)} fusion(bf16[1,1,4,2,2,384,384]{5,6,4,3,2,1,0:T(8,128)(2,1)} %collective-permute-done.2, bf16[1,1,4,2,2,384,384]{5,6,4,3,2,1,0:T(8,128)(2,1)} %collective-permute-done.3, f32[]{:T(128)} %bitcast.80, bf16[1,1,4,2,2,384,384]{5,6,4,3,2,1,0:T(8,128)(2,1)} %collective-permute-done, ...), kind=kLoop, calls=%fused_computation.9 | loop fusion | flops 16515072 | bytes 28311562 | tf_op jit(solution)/shard_map/add | solution.py:144
  419.3 6.6 %slice_bitcast_fusion = (f32[1,2,2,384,384]{3,4,2,1,0:T(8,128)S(1)}, f32[1,2,2,384,384]{3,4,2,1,0:T(8,128)}, f32[1,2,2,384,384]{3,4,2,1,0:T(8,128)}, f32[1,1,2,2,384,384]{4,5,3,2,1,0:T(8,128)S(1)}) fusion(f32[1,4,2,2,384,384]{4,5,3,2,1,0:T(8,128)} %add_bitcast_fusion), kind=kLoop, calls=%fused_computation.10 | loop fusion | bytes 18874368 | tf_op jit(solution)/shard_map/vmap()/squeeze | solution.py:123
  429.8 5.1 gather_fusion
  434.9 4.6 gather_fusion.1
  448.4 2.5 convolution_bitcast_fusion.5
  457.8 3.5 gather_fusion.3
  461.3 4.7 gather_fusion.2
  474.8 2.5 convolution_bitcast_fusion.3
  484.2 3.5 gather_fusion.5
  487.7 3.7 gather_fusion.4
  499.6 2.5 convolution_bitcast_fusion.1
  508.0 3.5 gather_fusion.7
  511.5 3.5 gather_fusion.6
  515.0 1.6 subtract_subtract_fusion
  522.8 1.8 maximum_bitcast_fusion
  524.6 4.9 all-to-all-start.1
  534.5 1.7 collective-permute-start.5
  537.6 33.5 %collective-permute-done.5 = bf16[1,1,1,2,384,384]{5,4,3,2,1,0:T(8,128)(2,1)S(1)} collective-permute-done((bf16[1,1,1,2,384,384]{5,4,3,2,1,0:T(8,128)(2,1)S(1)}, bf16[1,1,1,2,384,384]{5,4,3,2,1,0:T(8,128)(2,1)S(1)}, u32[]{:S(2)}, u32[]{:S(2)}) %collective-permute-start.5) | collective-permute-done | bytes 589856 | tf_op jit(solution)/shard_map/ppermute | solution.py:28
  571.1 11.5 %collective-permute-done.6 = bf16[1,1,1,2,384,384]{5,4,3,2,1,0:T(8,128)(2,1)S(1)} collective-permute-done((bf16[1,1,1,2,384,384]{5,4,3,2,1,0:T(8,128)(2,1)}, bf16[1,1,1,2,384,384]{5,4,3,2,1,0:T(8,128)(2,1)S(1)}, u32[]{:S(2)}, u32[]{:S(2)}) %collective-permute-start.6) | collective-permute-done | bytes 589856 | tf_op jit(solution)/shard_map/ppermute | solution.py:28
  583.4 1.6 maximum_bitcast_fusion.1
  585.0 2.3 gather_fusion.8
  587.3 4.3 copy.444
  (295 shorter events, 88.1 us)
Async XLA Ops:
  7.2 111.9 %all-gather.3.cloned.1.call-start = ((), (), s32[]{:S(2)}) async-start(), calls=%async_computation.2 | async-start | bytes 2949120 | tf_op jit(solution)/shard_map/all_gather | solution.py:172
  14.6 90.2 %copy-start.54 = (bf16[1,2,384,384]{3,2,1,0:T(8,128)(2,1)S(1)}, bf16[1,2,384,384]{3,2,1,0:T(8,128)(2,1)}, u32[]{:S(2)}) copy-start(bf16[1,2,384,384]{3,2,1,0:T(8,128)(2,1)} %param.13) | copy-start | bytes 1769476
  14.6 83.5 %all-to-all-start = ((bf16[1,4,1,2,2,384,384]{5,6,4,3,2,0,1:T(8,128)(2,1)}), bf16[1,4,1,2,2,384,384]{5,6,4,3,2,0,1:T(8,128)(2,1)}, u32[]{:S(2)}, u32[]{:S(2)}) async-start(bf16[1,4,1,2,2,384,384]{5,6,4,3,2,0,1:T(8,128)(2,1)} %copy.369), calls=%async_computation | async-start | bytes 9437184 | tf_op jit(solution)/shard_map/all_to_all | solution.py:168
  19.7 108.5 %all-gather.5.cloned.1.call-start = ((), (), s32[]{:S(2)}) async-start(), calls=%async_computation.3 | async-start | bytes 2949120 | tf_op jit(solution)/shard_map/all_gather | solution.py:173
  98.1 107.9 %collective-permute-start = (bf16[1,1,4,2,2,384,384]{5,6,4,3,2,1,0:T(8,128)(2,1)}, bf16[1,1,4,2,2,384,384]{5,6,4,3,2,1,0:T(8,128)(2,1)}, u32[]{:S(2)}, u32[]{:S(2)}) collective-permute-start(bf16[1,1,4,2,2,384,384]{5,6,4,3,2,1,0:T(8,128)(2,1)} %bitcast.79), channel_id=1, source_target_pairs={{0,1},{1,2},{2,3},{3,4},{4,5},{5,6},{6,7},{7,0},{8,9},{9,10},{10,1... | collective-permute-start | bytes 14155784 | tf_op jit(solution)/shard_map/ppermute | solution.py:35
  99.6 106.8 %collective-permute-start.1 = (bf16[1,1,4,2,2,384,384]{5,6,4,3,2,1,0:T(8,128)(2,1)}, bf16[1,1,4,2,2,384,384]{5,6,4,3,2,1,0:T(8,128)(2,1)}, u32[]{:S(2)}, u32[]{:S(2)}) collective-permute-start(bf16[1,1,4,2,2,384,384]{5,6,4,3,2,1,0:T(8,128)(2,1)} %bitcast.79), channel_id=1, source_target_pairs={{0,2},{1,3},{2,4},{3,5},{4,6},{5,7},{6,0},{7,1},{8,10},{9,11},{10,... | collective-permute-start | bytes 14155784 | tf_op jit(solution)/shard_map/ppermute | solution.py:35
  101.1 204.6 %collective-permute-start.2 = (bf16[1,1,4,2,2,384,384]{5,6,4,3,2,1,0:T(8,128)(2,1)}, bf16[1,1,4,2,2,384,384]{5,6,4,3,2,1,0:T(8,128)(2,1)}, u32[]{:S(2)}, u32[]{:S(2)}) collective-permute-start(bf16[1,1,4,2,2,384,384]{5,6,4,3,2,1,0:T(8,128)(2,1)} %bitcast.79), channel_id=1, source_target_pairs={{0,7},{1,0},{2,1},{3,2},{4,3},{5,4},{6,5},{7,6},{8,15},{9,8},{10,9... | collective-permute-start | bytes 14155784 | tf_op jit(solution)/shard_map/ppermute | solution.py:35
  104.3 303.0 %collective-permute-start.3 = (bf16[1,1,4,2,2,384,384]{5,6,4,3,2,1,0:T(8,128)(2,1)}, bf16[1,1,4,2,2,384,384]{5,6,4,3,2,1,0:T(8,128)(2,1)}, u32[]{:S(2)}, u32[]{:S(2)}) collective-permute-start(bf16[1,1,4,2,2,384,384]{5,6,4,3,2,1,0:T(8,128)(2,1)} %bitcast.79), channel_id=1, source_target_pairs={{0,6},{1,7},{2,0},{3,1},{4,2},{5,3},{6,4},{7,5},{8,14},{9,15},{10,... | collective-permute-start | bytes 14155784 | tf_op jit(solution)/shard_map/ppermute | solution.py:35
  108.1 3.5 copy-start.76
  108.1 8.7 %copy-start.78 = (f32[4]{0:T(128)S(1)}, f32[4]{0:T(128)}, u32[]{:S(2)}) copy-start(f32[4]{0:T(128)} %param.17) | copy-start | bytes 52
  108.2 8.7 %copy-start.79 = (s32[1,2]{1,0:T(1,128)S(1)}, s32[1,2]{1,0:T(1,128)}, u32[]{:S(2)}) copy-start(s32[1,2]{1,0:T(1,128)} %param.16) | copy-start | bytes 28
  137.3 288.8 %copy-start.22 = (f32[1,2,384,384]{2,3,1,0:T(8,128)}, f32[1,2,384,384]{2,3,1,0:T(8,128)S(1)}, u32[]{:S(2)}) copy-start(f32[1,2,384,384]{2,3,1,0:T(8,128)S(1)} %fusion.7) | copy-start | bytes 3538948
  434.9 5.3 copy-start.55
  447.7 3.1 copy-start.28
  453.7 2.5 copy-start.2
  453.7 2.5 copy-start.50
  453.7 2.6 copy-start.51
  461.3 5.3 copy-start.56
  474.1 3.1 copy-start.30
  480.1 2.5 copy-start
  480.1 2.6 copy-start.49
  487.7 3.7 copy-start.57
  498.9 3.1 copy-start.32
  518.5 2.9 copy-start.24
  518.5 2.9 copy-start.26
  524.6 4.9 copy-start.25
  524.6 4.9 copy-start.27
  524.6 62.7 %all-to-all-start.1 = ((bf16[1,1,4,2,384,384]{4,5,3,1,0,2:T(8,128)(2,1)}), bf16[1,1,4,2,384,384]{4,5,3,1,0,2:T(8,128)(2,1)}, u32[]{:S(2)}, u32[]{:S(2)}) async-start(bf16[1,1,4,2,384,384]{4,5,3,1,0,2:T(8,128)(2,1)} %maximum_bitcast_fusion), calls=%async_computation.1 | async-start | bytes 4718592 | tf_op jit(solution)/shard_map/all_to_all | solution.py:186
  533.7 3.9 collective-permute-start.4
  534.5 36.6 %collective-permute-start.5 = (bf16[1,1,1,2,384,384]{5,4,3,2,1,0:T(8,128)(2,1)S(1)}, bf16[1,1,1,2,384,384]{5,4,3,2,1,0:T(8,128)(2,1)S(1)}, u32[]{:S(2)}, u32[]{:S(2)}) collective-permute-start(bf16[1,1,1,2,384,384]{5,4,3,2,1,0:T(8,128)(2,1)S(1)} %bitcast.1093), channel_id=1, source_target_pairs={{0,16},{8,24},{16,0},{24,8},{1,17},{9,25},{17,1},{25,9},{2,18},{10... | collective-permute-start | bytes 1769480 | tf_op jit(solution)/shard_map/ppermute | solution.py:28
  537.3 45.3 %collective-permute-start.6 = (bf16[1,1,1,2,384,384]{5,4,3,2,1,0:T(8,128)(2,1)}, bf16[1,1,1,2,384,384]{5,4,3,2,1,0:T(8,128)(2,1)S(1)}, u32[]{:S(2)}, u32[]{:S(2)}) collective-permute-start(bf16[1,1,1,2,384,384]{5,4,3,2,1,0:T(8,128)(2,1)} %bitcast.374), channel_id=1, source_target_pairs={{0,24},{8,16},{16,8},{24,0},{1,25},{9,17},{17,9},{25,1},{2,26},{10... | collective-permute-start | bytes 1769480 | tf_op jit(solution)/shard_map/ppermute | solution.py:28
  571.1 11.5 %copy-start.72 = (bf16[1,1,1,2,384,384]{5,4,3,2,1,0:T(8,128)(2,1)}, bf16[1,1,1,2,384,384]{5,4,3,2,1,0:T(8,128)(2,1)S(1)}, u32[]{:S(2)}) copy-start(bf16[1,1,1,2,384,384]{5,4,3,2,1,0:T(8,128)(2,1)S(1)} %collective-permute-done.5) | copy-start | bytes 1769476
  (59 other events, 77.3 us)
Sparse Core Ops, SparseCore 0:
  9.5 37.9 all-gather.2
  49.1 35.9 all-gather.4
